TPU v7x, 32 devices: a whole 2x2x4 slice. The times are simulated.
32 devices in a mesh: grp: 8 (over y, x, core), top: 4 (over z).
Axes of the slice: x: 2, y: 2, z: 4, core: 2. Of those that a mesh axis runs over, the one named last changes fastest.
Arguments:
- basis_grad: float32 [8, 4, 512, 384], P('grp', 'top'), may hold values from -6 to 6
- leaf_q: float32 [8, 4, 512, 384], P('grp', 'top'), may hold values from -0.25 to 0.25
- leaf_rinv: float32 [8, 4, 384, 384], P('grp', 'top'), may hold values from -5 to 4, as said below
- merge_q1: float32 [8, 4, 384, 384], P('grp', 'top'), may hold values from -0.3125 to 0.3125
- merge_q2: float32 [4, 384, 384], P('top', 'grp'), may hold values from -0.15625 to 0.15625
Outputs:
- data_grad: float32 [8, 4, 512, 384], P('grp', 'top')
Inputs may be any that keep to these rules, and one draw needn't show every extreme that they name: Each leaf_rinv[i,g] is upper triangular with a diagonal between 1 and 4.
All inputs are finite; a program needn't handle non-finite values.
Results may differ from a plain program's by a relative error of at most 0.00023.
Values sent between devices are 32-bit elements; how exact they have to be, the bound alone decides.
A program may use at most 64 MiB of HBM per device.

v0:
```python
import jax
import jax.numpy as jnp
from jax import lax
from jax.sharding import PartitionSpec as P

highest = lax.Precision.HIGHEST


def product(former, latter, former_dim, latter_dim):
    return lax.dot_general(
        former,
        latter,
        (((former_dim,), (latter_dim,)), ((), ())),
        precision=highest,
        preferred_element_type=jnp.float32,
    )


def symmetrize(matrix):
    return jnp.tril(matrix) + jnp.tril(matrix, -1).T


def per_device(basis_grad, leaf_q, leaf_rinv, merge_q1, merge_q2):
    cotangent = basis_grad[0, 0]
    leaf_basis = leaf_q[0, 0]
    inverse = leaf_rinv[0, 0]
    first_block = merge_q1[0, 0]
    second_factor = lax.all_gather(merge_q2[0], "grp", axis=0, tiled=True)
    projected = product(leaf_basis, cotangent, 0, 0)
    combined = product(first_block, second_factor, 1, 0)
    leaf_cotan = product(cotangent, combined, 1, 1)
    first_cotan = product(projected, second_factor, 1, 1)
    second_term = product(first_block, projected, 0, 0)
    gram_term = product(first_cotan, first_block, 0, 0)
    second_cotan, group_gram = lax.psum((second_term, gram_term), "grp")
    top_adjoint = lax.psum(-product(second_cotan, second_factor, 0, 0), "top")
    top_sym = symmetrize(top_adjoint)
    group_back = product(second_cotan + product(second_factor, top_sym, 1, 0), second_factor, 1, 1)
    group_adjoint = group_back.T - group_gram
    group_sym = symmetrize(group_adjoint)
    leaf_back = product(first_cotan + product(first_block, group_sym, 1, 0), first_block, 1, 1)
    leaf_adjoint = leaf_back.T - product(leaf_cotan, leaf_basis, 0, 0)
    leaf_sym = symmetrize(leaf_adjoint)
    inner = leaf_cotan + product(leaf_basis, leaf_sym, 1, 0)
    result = product(inner, inverse, 1, 1)
    return result[None, None]


def solution(mesh):
    placed = (
        P("grp", "top", None, None),
        P("grp", "top", None, None),
        P("grp", "top", None, None),
        P("grp", "top", None, None),
        P("top", "grp", None),
    )
    return jax.shard_map(
        per_device,
        mesh=mesh,
        in_specs=placed,
        out_specs=P("grp", "top", None, None),
        check_vma=False,
    )
```

profile of v0, /device:TPU:1, one launch (start us, length us, event | category | flops | bytes accessed | tf_op | source)
XLA Modules:
  0.0 152.7 jit_solution(6126031068514458693)
XLA Ops:
  6.5 11.8 %all-gather = f32[1,384,384]{2,1,0:T(8,128)S(1)} all-gather(f32[1,48,384]{2,1,0:T(8,128)} %param.9), channel_id=2, replica_groups=mesh['grp'=8,'top'=4] {'grp'}, dimensions={1}, use_global_device_ids=true | all-gather | bytes 663552 | tf_op jit(solution)/shard_map/all_gather | solution.py:28
  18.3 2.6 %fusion.6 = f32[384,384]{1,0:T(8,128)S(1)} fusion(f32[1,1,512,384]{3,2,1,0:T(8,128)S(1)} %copy-done, f32[1,1,512,384]{3,2,1,0:T(8,128)} %param.5), kind=kOutput, calls=%fused_computation.13 | convolution fusion | flops 905969664 | bytes 2162688 | tf_op jit(solution)/shard_map/dot_general | solution.py:10
  20.9 1.3 fusion.20
  22.2 2.1 %convolution_bitcast_fusion.4 = f32[384,384]{0,1:T(8,128)} fusion(f32[384,384]{1,0:T(8,128)S(1)} %fusion.6, f32[1,1,384,384]{3,2,1,0:T(8,128)S(1)} %copy-done.1), kind=kOutput, calls=%fused_computation.9 | convolution fusion | flops 679477248 | bytes 1769472 | tf_op jit(solution)/shard_map/dot_general | solution.py:10
  24.3 2.2 %fusion.27 = f32[384,384]{1,0:T(8,128)} fusion(f32[384,384]{1,0:T(8,128)S(1)} %fusion.20, f32[1,1,384,384]{3,2,1,0:T(8,128)S(1)} %copy-done.1), kind=kOutput, calls=%fused_computation.36 | convolution fusion | flops 679477248 | bytes 1769472 | tf_op jit(solution)/shard_map/dot_general | solution.py:10
  26.5 0.0 all-reduce.6.cloned.1.call-update
  26.5 0.2 all-reduce.4.cloned.1.call-start
  26.7 2.1 %fusion.22 = f32[384,384]{1,0:T(8,128)} fusion(f32[1,384,384]{2,1,0:T(8,128)S(1)} %all-gather, f32[1,1,384,384]{3,2,1,0:T(8,128)S(1)} %copy-done.1), kind=kOutput, calls=%fused_computation.31 | convolution fusion | flops 679477248 | bytes 1769472 | tf_op jit(solution)/shard_map/dot_general | solution.py:10
  28.8 53.8 %all-reduce.6.cloned.1.call-done = (f32[384,384]{1,0:T(8,128)}, f32[384,384]{0,1:T(8,128)}) async-done(((f32[384,384]{1,0:T(8,128)}, f32[384,384]{0,1:T(8,128)}), (f32[384,384]{1,0:T(8,128)}, f32[384,384]{0,1:T(8,128)})) %all-reduce.6.cloned.1.call-update) | async-done | bytes 1179664 | tf_op jit(solution)/shard_map/psum | solution.py:35
  82.7 3.1 %convolution_negate_fusion = f32[384,384]{1,0:T(8,128)} fusion(f32[384,384]{0,1:T(8,128)} %get-tuple-element.6, f32[1,384,384]{2,1,0:T(8,128)S(1)} %all-gather), kind=kOutput, calls=%fused_computation.8 | convolution fusion | flops 679624704 | bytes 1769472 | tf_op jit(solution)/shard_map/dot_general | solution.py:10
  85.8 2.7 %fusion.9 = f32[384,512]{1,0:T(8,128)S(1)} fusion(f32[384,384]{1,0:T(8,128)} %fusion.22, f32[1,1,512,384]{3,2,1,0:T(8,128)} %param.5), kind=kOutput, calls=%fused_computation.16 | convolution fusion | flops 905969664 | bytes 2162688 | tf_op jit(solution)/shard_map/dot_general | solution.py:10
  88.6 2.2 %fusion.4 = f32[384,384]{1,0:T(8,128)} fusion(f32[384,512]{1,0:T(8,128)S(1)} %fusion.9, f32[1,1,512,384]{3,2,1,0:T(8,128)S(1)} %copy-done), kind=kOutput, calls=%fused_computation.11 | convolution fusion | flops 905969664 | bytes 2162688 | tf_op jit(solution)/shard_map/dot_general | solution.py:10
  90.8 2.1 %copy.11 = f32[384,384]{0,1:T(8,128)} copy(f32[384,384]{1,0:T(8,128)} %fusion.4) | data formatting | bytes 1179648 | tf_op jit(solution)/shard_map/dot_general | solution.py:10
  93.0 32.0 %all-reduce.4.cloned.1.call-done = f32[384,384]{1,0:T(8,128)} async-done(((f32[384,384]{1,0:T(8,128)}), f32[384,384]{1,0:T(8,128)}) %all-reduce.4.cloned.1.call-update) | async-done | bytes 589840 | tf_op jit(solution)/shard_map/psum | solution.py:36
  124.9 2.1 %copy.6 = f32[384,384]{0,1:T(8,128)} copy(f32[384,384]{1,0:T(8,128)} %all-reduce.4.cloned.1.call-done) | data formatting | bytes 1179648 | tf_op jit(solution)/shard_map/psum | solution.py:36
  127.0 2.8 %fusion.2 = f32[384,384]{0,1:T(8,128)S(1)} fusion(f32[384,384]{0,1:T(8,128)} %get-tuple-element.6, f32[1,384,384]{2,1,0:T(8,128)S(1)} %all-gather, f32[384,384]{1,0:T(8,128)} %all-reduce.4.cloned.1.call-done, f32[384,384]{0,1:T(8,128)} %copy.6, s32[384]{0:T(512)S(1)} %iota_add_fusion), kind=kOutput, calls=%fused_computation.7 | convolution fusion | flops 680361984 | bytes 2950656 | tf_op jit(solution)/shard_map/dot_general | solution.py:10
  129.9 2.1 %fusion.1 = f32[384,384]{1,0:T(8,128)} fusion(f32[384,384]{1,0:T(8,128)S(1)} %copy-done.6, f32[384,384]{0,1:T(8,128)S(1)} %fusion.2, f32[1,384,384]{2,1,0:T(8,128)S(1)} %all-gather), kind=kOutput, calls=%fused_computation.5 | convolution fusion | flops 679624704 | bytes 2359296 | tf_op jit(solution)/shard_map/dot_general | solution.py:10
  132.0 2.2 %copy.9 = f32[384,384]{0,1:T(8,128)} copy(f32[384,384]{1,0:T(8,128)} %fusion.1) | data formatting | bytes 1179648 | tf_op jit(solution)/shard_map/sub | solution.py:39
  134.2 2.5 %fusion = f32[384,384]{1,0:T(8,128)S(1)} fusion(f32[384,384]{1,0:T(8,128)S(1)} %fusion.20, f32[1,1,384,384]{3,2,1,0:T(8,128)S(1)} %copy-done.1, f32[384,384]{1,0:T(8,128)S(1)} %copy-done.2, f32[384,384]{0,1:T(8,128)} %copy.9, s32[384]{0:T(512)S(1)} %iota_add_fusion), kind=kOutput, calls=%fused_computation.3 | convolution fusion | flops 680361984 | bytes 2950656 | tf_op jit(solution)/shard_map/dot_general | solution.py:10
  136.7 1.3 fusion.24
  138.0 1.1 copy.12
  139.0 0.4 copy-done.4
  139.4 2.9 %convolution_add_fusion = f32[384,512]{1,0:T(8,128)S(1)} fusion(f32[384,512]{1,0:T(8,128)S(1)} %fusion.9, f32[1,1,512,384]{3,2,1,0:T(8,128)S(1)} %copy-done, f32[384,384]{0,1:T(8,128)} %copy.12, f32[384,384]{1,0:T(8,128)S(1)} %copy-done.3, f32[384,384]{0,1:T(8,128)S(1)} %copy-done.4, f32[384,384]{1,0:T(8,128)S(1)} %fusion.24, s32[384]{0:T(512)S(1)} %iota_add_fusion), kind=kOutput, calls=%fused_computation.1 | convolution fusion | flops 907198464 | bytes 4720128 | tf_op jit(solution)/shard_map/dot_general | solution.py:10
  142.3 3.5 %convolution_bitcast_fusion = f32[1,1,512,384]{3,2,1,0:T(8,128)} fusion(f32[384,512]{1,0:T(8,128)S(1)} %convolution_add_fusion, f32[1,1,384,384]{3,2,1,0:T(8,128)S(1)} %copy-done.5), kind=kOutput, calls=%fused_computation | convolution fusion | flops 905969664 | bytes 2162688 | tf_op jit(solution)/shard_map/dot_general | solution.py:10
  (16 shorter events, 0.0 us)
Async XLA Ops:
  6.5 11.8 %copy-start = (f32[1,1,512,384]{3,2,1,0:T(8,128)S(1)}, f32[1,1,512,384]{3,2,1,0:T(8,128)}, u32[]{:S(2)}) copy-start(f32[1,1,512,384]{3,2,1,0:T(8,128)} %param.6) | copy-start | bytes 2359300
  6.5 76.1 %all-reduce.6.cloned.1.call-start = ((), (), s32[]{:S(2)}) async-start(), calls=%async_computation.1 | async-start | bytes 2359296 | tf_op jit(solution)/shard_map/psum | solution.py:35
  20.9 1.3 copy-start.1
  26.5 98.4 %all-reduce.4.cloned.1.call-start = ((), (), s32[]{:S(2)}) async-start(), calls=%async_computation | async-start | bytes 1179648 | tf_op jit(solution)/shard_map/psum | solution.py:36
  127.0 2.9 %copy-start.6 = (f32[384,384]{1,0:T(8,128)S(1)}, f32[384,384]{1,0:T(8,128)}, u32[]{:S(2)}) copy-start(f32[384,384]{1,0:T(8,128)} %get-tuple-element.5) | copy-start | bytes 1769476
  132.0 2.2 %copy-start.2 = (f32[384,384]{1,0:T(8,128)S(1)}, f32[384,384]{1,0:T(8,128)}, u32[]{:S(2)}) copy-start(f32[384,384]{1,0:T(8,128)} %fusion.1) | copy-start | bytes 1769476
  137.9 1.1 copy-start.3
  137.9 1.4 copy-start.4
  139.4 2.9 %copy-start.5 = (f32[1,1,384,384]{3,2,1,0:T(8,128)S(1)}, f32[1,1,384,384]{3,2,1,0:T(8,128)}, u32[]{:S(2)}) copy-start(f32[1,1,384,384]{3,2,1,0:T(8,128)} %param.7) | copy-start | bytes 1769476
Sparse Core Ops, SparseCore 0:
  26.6 55.9 all-reduce.5
  85.9 38.9 all-reduce.3
where the time goes:
time: 154 us; the launch traced here: 153 us
  waiting for transfers between devices  85.8 us (56%)
  matrix products  33.4 us (22%)
  between operations  13.5 us (9%)
  blocking collectives  11.8 us (8%)
  local copies, waits for them, and re-layouts  7.89 us (5%)
    psum x1, waiting for transfers between devices, per_device(): second_cotan, group_gram = lax.psum((second_term, gram_term), 'grp')  53.8 us
    dot_general x14, matrix products, product(): lax.dot_general(former, latter, (((former_dim,), (latter_dim,)), ((), ())...  33.4 us
    psum x1, waiting for transfers between devices, per_device(): top_adjoint = lax.psum(-product(second_cotan, second_factor, 0, 0), 'top')  32 us
    all_gather x1, blocking collectives, per_device(): second_factor = lax.all_gather(merge_q2[0], 'grp', axis=0, tiled=True)  11.8 us
    dot_general x2, local copies, waits for them, and re-layouts, product(): lax.dot_general(former, latter, (((former_dim,), (latter_dim,)), ((), ())...  3.18 us
  transfers between devices with their start and end apart: 2, of which 2 were waited for; matrix products, arithmetic and copies ran while one was open for 6% of the time, Pallas kernels for 0%

commit v1 on v0

v1 whole, which is shorter than its diff:
```python
import jax
import jax.numpy as jnp
from jax import lax
from jax.sharding import PartitionSpec as P


def product(former, latter, former_dim, latter_dim):
    return lax.dot_general(
        former,
        latter,
        (((former_dim,), (latter_dim,)), ((), ())),
        precision=lax.Precision.HIGH,
        preferred_element_type=jnp.float32,
    )


def symmetrize(matrix):
    return jnp.tril(matrix) + jnp.tril(matrix, -1).T


def per_device(basis_grad, leaf_q, leaf_rinv, merge_q1, merge_q2):
    cotangent = basis_grad[0, 0]
    leaf_basis = leaf_q[0, 0]
    inverse = leaf_rinv[0, 0]
    first_block = merge_q1[0, 0]
    second_factor = lax.all_gather(merge_q2[0], "grp", axis=0, tiled=True)
    projected = product(leaf_basis, cotangent, 0, 0)
    combined = product(first_block, second_factor, 1, 0)
    top_adjoint = -lax.psum(product(projected, combined, 0, 0), ("grp", "top"))
    top_sym = symmetrize(top_adjoint)
    spread = product(leaf_basis, combined, 1, 0)
    outer = product(inverse, combined, 1, 0)
    inner = cotangent + product(spread, top_sym, 1, 0)
    result = product(inner, outer, 1, 1)
    return result[None, None]


def solution(mesh):
    placed = (
        P("grp", "top", None, None),
        P("grp", "top", None, None),
        P("grp", "top", None, None),
        P("grp", "top", None, None),
        P("top", "grp", None),
    )
    return jax.shard_map(
        per_device,
        mesh=mesh,
        in_specs=placed,
        out_specs=P("grp", "top", None, None),
        check_vma=False,
    )
```

time: 154 us -> 164 us (1.065)
  waiting for transfers between devices: 85.8 us -> 124 us
  matrix products: 33.4 us -> 9.86 us
  local copies, waits for them, and re-layouts: 7.89 us -> 2.51 us
    psum x2 -> x1, waiting for transfers between devices: 85.8 us -> 124 us  [per_device(): top_adjoint = -lax.psum(product(projected, combined, 0, 0), ('grp', 'top'))]
    dot_general x14 -> x7, matrix products: 33.4 us -> 9.86 us  [product(): lax.dot_general(former, latter, (((former_dim,), (latter_dim,)), ((), ())...]
    dot_general x2 -> x0, local copies, waits for them, and re-layouts: 3.18 us -> none  [product(): lax.dot_general(former, latter, (((former_dim,), (latter_dim,)), ((), ())...]
    sub x1 -> x0, local copies, waits for them, and re-layouts: 2.19 us -> none  [per_device(): group_adjoint = group_back.T - group_gram]
    psum x1 -> x0, local copies, waits for them, and re-layouts: 2.11 us -> none  [per_device(): top_adjoint = lax.psum(-product(second_cotan, second_factor, 0, 0), 'top')]
  transfers between devices with their start and end apart: 2 -> 1, of which waited for: 2 -> 1; matrix products, arithmetic and copies ran while one was open for 6% -> 1% of each run, Pallas kernels for 0% -> 0%
where the time goes in v1:
time: 164 us; the launch traced here: 163 us
  waiting for transfers between devices  124 us (76%)
  between operations  13.5 us (8%)
  blocking collectives  11.8 us (7%)
  matrix products  9.86 us (6%)
  local copies, waits for them, and re-layouts  2.51 us (2%)
    psum x1, waiting for transfers between devices, per_device(): top_adjoint = -lax.psum(product(projected, combined, 0, 0), ('grp', 'top'))  124 us
    all_gather x1, blocking collectives, per_device(): second_factor = lax.all_gather(merge_q2[0], 'grp', axis=0, tiled=True)  11.8 us
    dot_general x7, matrix products, product(): lax.dot_general(former, latter, (((former_dim,), (latter_dim,)), ((), ())...  9.86 us
  transfers between devices with their start and end apart: 1, of which 1 were waited for; matrix products, arithmetic and copies ran while one was open for 1% of the time, Pallas kernels for 0%

profile of v1, /device:TPU:1, one launch (start us, length us, event | category | flops | bytes accessed | tf_op | source)
XLA Modules:
  0.0 163.1 jit_solution(13517483141683757118)
XLA Ops:
  6.5 0.0 copy-start
  6.5 0.0 copy-start.2
  6.5 0.0 all-reduce.2.cloned.1.call-start
  6.5 11.8 %all-gather = f32[1,384,384]{2,1,0:T(8,128)S(1)} all-gather(f32[1,48,384]{2,1,0:T(8,128)} %param.9), channel_id=2, replica_groups=mesh['grp'=8,'top'=4] {'grp'}, dimensions={1}, use_global_device_ids=true | all-gather | bytes 663552 | tf_op jit(solution)/shard_map/all_gather | solution.py:26
  18.3 0.0 copy-done.2
  18.3 0.0 copy-start.1
  18.3 0.7 fusion.7
  19.1 0.0 copy-done
  19.1 0.4 copy-done.1
  19.5 0.8 fusion
  20.3 1.6 fusion.17
  21.9 0.0 copy-start.3
  21.9 0.0 all-reduce.2.cloned.1.call-update
  21.9 1.0 copy-done.3
  22.9 1.1 fusion.5
  24.1 1.2 fusion.2
  25.2 124.3 %all-reduce.2.cloned.1.call-done = f32[384,384]{1,0:T(8,128)} async-done(((f32[384,384]{1,0:T(8,128)}), f32[384,384]{1,0:T(8,128)}) %all-reduce.2.cloned.1.call-update) | async-done | bytes 589840 | tf_op jit(solution)/shard_map/psum | solution.py:29
  149.6 1.1 neg.3
  150.7 1.1 copy.6
  151.7 2.7 %convolution_add_fusion = f32[512,384]{1,0:T(8,128)S(1)} fusion(f32[384,512]{1,0:T(8,128)S(1)} %fusion.2, f32[1,1,512,384]{3,2,1,0:T(8,128)S(1)} %copy-done.1, f32[384,384]{0,1:T(8,128)} %copy.6, s32[384]{0:T(512)S(1)} %iota_add_fusion, f32[384,384]{1,0:T(8,128)} %all-reduce.2.cloned.1.call-done), kind=kOutput, calls=%fused_computation.1 | convolution fusion | flops 454066176 | bytes 3540480 | tf_op jit(solution)/shard_map/dot_general | solution.py:8
  154.5 1.8 %convolution_bitcast_fusion = f32[1,1,512,384]{3,2,1,0:T(8,128)} fusion(f32[512,384]{1,0:T(8,128)S(1)} %convolution_add_fusion, f32[384,384]{1,0:T(8,128)S(1)} %fusion.5), kind=kOutput, calls=%fused_computation | convolution fusion | flops 452984832 | bytes 2162688 | tf_op jit(solution)/shard_map/dot_general | solution.py:8
  (1 shorter events, 0.0 us)
Async XLA Ops:
  6.5 12.5 %copy-start = (f32[1,1,512,384]{3,2,1,0:T(8,128)S(1)}, f32[1,1,512,384]{3,2,1,0:T(8,128)}, u32[]{:S(2)}) copy-start(f32[1,1,512,384]{3,2,1,0:T(8,128)} %param.6) | copy-start | bytes 2359300
  6.5 11.8 %copy-start.2 = (f32[1,1,384,384]{3,2,1,0:T(8,128)S(1)}, f32[1,1,384,384]{3,2,1,0:T(8,128)}, u32[]{:S(2)}) copy-start(f32[1,1,384,384]{3,2,1,0:T(8,128)} %param.8) | copy-start | bytes 1769476
  6.5 143.0 %all-reduce.2.cloned.1.call-start = ((), (), s32[]{:S(2)}) async-start(), calls=%async_computation | async-start | bytes 1179648 | tf_op jit(solution)/shard_map/psum | solution.py:29
  18.3 1.1 copy-start.1
  21.9 1.1 copy-start.3
Sparse Core Ops, SparseCore 0:
  22.0 127.5 all-reduce.1

commit v2 on v1

v2 whole, which is shorter than its diff:
```python
import functools

import jax
import jax.numpy as jnp
from jax import lax
from jax.experimental import pallas as pl
from jax.experimental.pallas import tpu as pltpu
from jax.sharding import PartitionSpec as P

MESH = pl.DeviceIdType.MESH
TILE = 128
f32 = jnp.float32
bf16 = jnp.bfloat16


def split(value, high, low):
    top = value.astype(bf16)
    high[...] = top
    low[...] = (value - top.astype(f32)).astype(bf16)


def dot(former, latter, latter_dim):
    return lax.dot_general(
        former, latter, (((1,), (latter_dim,)), ((), ())), preferred_element_type=f32
    )


def product(former, latter, latter_dim=0):
    former_high, former_low = former
    latter_high, latter_low = latter
    total = dot(former_high[...], latter_low[...], latter_dim)
    total += dot(former_low[...], latter_high[...], latter_dim)
    return total + dot(former_high[...], latter_high[...], latter_dim)


def kernel(
    n, m,
    b_hbm, q_hbm, r_hbm, m1_hbm, m2_hbm, o_ref,
    b, q, r, m1, m2_parts, m2,
    bh, bl, bth, btl, qh, ql, rh, rl, m1h, m1l, m2h, m2l,
    wh, wl, ch, cl, dh, dl, th, tl, yh, yl,
    packed, scatter, slab_sum, across, total,
    load_sem, m2_send, m2_recv, rs_send, rs_recv, z_send, z_recv, ag_send, ag_recv,
):
    me = lax.axis_index("grp")
    my_top = lax.axis_index("top")
    width = m1.shape[0]
    blocks = width // TILE
    part = m2_parts.shape[1]
    slab = slab_sum.shape[0]

    loads = [
        pltpu.make_async_copy(src, dst, load_sem.at[at])
        for at, (src, dst) in enumerate(
            (
                (b_hbm.at[0, 0], b),
                (q_hbm.at[0, 0], q),
                (m1_hbm.at[0, 0], m1),
                (r_hbm.at[0, 0], r),
                (m2_hbm.at[0], m2_parts.at[me]),
            )
        )
    ]
    for load in loads:
        load.start()

    barrier = pltpu.get_barrier_semaphore()
    for k in range(1, n):
        pl.semaphore_signal(
            barrier, inc=1, device_id={"grp": lax.rem(me + k, n)}, device_id_type=MESH
        )
    for k in range(1, m):
        pl.semaphore_signal(
            barrier, inc=1, device_id={"top": lax.rem(my_top + k, m)}, device_id_type=MESH
        )
    pl.semaphore_wait(barrier, n + m - 2)

    def spread(axis, at, size, source, target, send, recv):
        copies = []
        for k in range(1, size):
            peer = lax.rem(at + k, size)
            copy = pltpu.make_async_remote_copy(
                src_ref=source(peer),
                dst_ref=target(k),
                send_sem=send.at[k - 1],
                recv_sem=recv.at[k - 1],
                device_id={axis: peer},
                device_id_type=MESH,
            )
            copy.start()
            copies.append(copy)
        return copies

    gather = spread(
        "grp", me, n, lambda peer: m2_hbm.at[0], lambda k: m2_parts.at[me], m2_send, m2_recv
    )

    loads[0].wait()
    split(b[...].T, bth, btl)
    loads[1].wait()
    split(q[...], qh, ql)
    split(product((bth, btl), (qh, ql)), wh, wl)
    loads[2].wait()
    split(m1[...], m1h, m1l)
    split(product((wh, wl), (m1h, m1l)), wh, wl)

    loads[4].wait()
    for copy in gather:
        copy.wait_recv()
    for j in range(n):
        m2[j * part:(j + 1) * part, :] = m2_parts[j]
    split(m2[...], m2h, m2l)
    for i in range(blocks):
        rows = pl.ds(i * TILE, TILE)
        columns = pl.ds(0, (i + 1) * TILE)
        row = product(
            (wh.at[rows, :], wl.at[rows, :]), (m2h.at[:, columns], m2l.at[:, columns])
        )
        for j in range(i + 1):
            packed[pl.ds((i * (i + 1) // 2 + j) * TILE, TILE), :] = row[:, j * TILE:(j + 1) * TILE]

    def part_of(ref, at):
        return ref.at[pl.ds(pl.multiple_of(at * slab, 8), slab), :]

    reduce = spread(
        "grp", me, n, lambda peer: part_of(packed, peer), lambda k: scatter.at[k - 1], rs_send, rs_recv
    )
    split(product((m1h, m1l), (m2h, m2l)), ch, cl)
    value = packed[pl.ds(pl.multiple_of(me * slab, 8), slab), :]
    for k, copy in enumerate(reduce):
        copy.wait_recv()
        value += scatter[k]
    slab_sum[...] = value
    over = spread(
        "top", my_top, m, lambda peer: slab_sum, lambda k: across.at[k - 1], z_send, z_recv
    )
    split(product((qh, ql), (ch, cl)), yh, yl)
    for k, copy in enumerate(over):
        copy.wait_recv()
        value += across[k]
    total[pl.ds(pl.multiple_of(me * slab, 8), slab), :] = value
    share = spread(
        "grp", me, n, lambda peer: part_of(total, me), lambda k: part_of(total, me), ag_send, ag_recv
    )
    loads[3].wait()
    split(r[...], rh, rl)
    split(product((rh, rl), (ch, cl)), dh, dl)
    split(b[...], bh, bl)
    o_ref[...] = product((bh, bl), (dh, dl), 1)
    for copy in share:
        copy.wait_recv()

    row_at = lax.broadcasted_iota(jnp.int32, (TILE, TILE), 0)
    column_at = lax.broadcasted_iota(jnp.int32, (TILE, TILE), 1)
    for i in range(blocks):
        for j in range(i + 1):
            block = -total[pl.ds((i * (i + 1) // 2 + j) * TILE, TILE), :]
            if i == j:
                block = jnp.where(row_at >= column_at, block, block.T)
            here = (pl.ds(i * TILE, TILE), pl.ds(j * TILE, TILE))
            split(block, th.at[here], tl.at[here])
            if i != j:
                there = (pl.ds(j * TILE, TILE), pl.ds(i * TILE, TILE))
                split(block.T, th.at[there], tl.at[there])
    split(product((dh, dl), (th, tl)), wh, wl)
    o_ref[...] += product((yh, yl), (wh, wl), 1)

    for copies in (gather, reduce, over, share):
        for copy in copies:
            copy.wait_send()


def per_device(n, m, basis_grad, leaf_q, leaf_rinv, merge_q1, merge_q2):
    rows, width = basis_grad.shape[2:]
    part = merge_q2.shape[1]
    blocks = width // TILE
    length = blocks * (blocks + 1) // 2 * TILE
    slab = length // n
    square, tall = (width, width), (rows, width)

    def pair(shape):
        return [pltpu.VMEM(shape, bf16)] * 2

    def semaphores(count):
        return pltpu.SemaphoreType.DMA((max(count, 1),))

    result = pl.pallas_call(
        functools.partial(kernel, n, m),
        out_shape=jax.ShapeDtypeStruct(tall, f32),
        in_specs=[pl.BlockSpec(memory_space=pl.ANY)] * 5,
        out_specs=pl.BlockSpec(memory_space=pltpu.VMEM),
        scratch_shapes=[
            pltpu.VMEM(tall, f32),
            pltpu.VMEM(tall, f32),
            pltpu.VMEM(square, f32),
            pltpu.VMEM(square, f32),
            pltpu.VMEM((n, part, width), f32),
            pltpu.VMEM(square, f32),
            *pair(tall), *pair((width, rows)), *pair(tall), *pair(square), *pair(square), *pair(square),
            *pair(square), *pair(square), *pair(square), *pair(square), *pair(tall),
            pltpu.VMEM((length, TILE), f32),
            pltpu.VMEM((n - 1, slab, TILE), f32),
            pltpu.VMEM((slab, TILE), f32),
            pltpu.VMEM((m - 1, slab, TILE), f32),
            pltpu.VMEM((length, TILE), f32),
            semaphores(5),
            *[semaphores(n - 1)] * 4,
            *[semaphores(m - 1)] * 2,
            *[semaphores(n - 1)] * 2,
        ],
        compiler_params=pltpu.CompilerParams(
            collective_id=0, has_side_effects=True, vmem_limit_bytes=48 * 1024 * 1024
        ),
    )(basis_grad, leaf_q, leaf_rinv, merge_q1, merge_q2)
    return result[None, None]


def solution(mesh):
    placed = (
        P("grp", "top", None, None),
        P("grp", "top", None, None),
        P("grp", "top", None, None),
        P("grp", "top", None, None),
        P("top", "grp", None),
    )
    return jax.shard_map(
        functools.partial(per_device, mesh.shape["grp"], mesh.shape["top"]),
        mesh=mesh,
        in_specs=placed,
        out_specs=P("grp", "top", None, None),
        check_vma=False,
    )
```

time: 164 us -> 40.2 us (0.25)
  waiting for transfers between devices: 124 us -> 0 us
  Pallas kernels: 0 us -> 33.6 us
  between operations: 13.5 us -> 0.01 us
  blocking collectives: 11.8 us -> 0 us
  matrix products: 9.86 us -> 0 us
  local copies, waits for them, and re-layouts: 2.51 us -> 6.16 us
    psum x1 -> x0, waiting for transfers between devices: 124 us -> none  [per_device(): top_adjoint = -lax.psum(product(projected, combined, 0, 0), ('grp', 'top'))]
    pallas_call x0 -> x1, Pallas kernels: none -> 33.6 us  [per_device(): pl.pallas_call(functools.partial(kernel, n, m), out_shape=jax.ShapeDtypeS...]
    all_gather x1 -> x0, blocking collectives: 11.8 us -> none  [per_device(): second_factor = lax.all_gather(merge_q2[0], 'grp', axis=0, tiled=True)]
    dot_general x7 -> x0, matrix products: 9.86 us -> none  [product(): lax.dot_general(former, latter, (((former_dim,), (latter_dim,)), ((), ())...]
    unnamed x8 -> x11, local copies, waits for them, and re-layouts: 1.46 us -> 6.16 us
  transfers between devices with their start and end apart: 1 -> 0, of which waited for: 1 -> 0; matrix products, arithmetic and copies ran while one was open for 1% -> 0% of each run, Pallas kernels for 0% -> 0%
where the time goes in v2:
time: 40.2 us; the launch traced here: 39.8 us
  Pallas kernels  33.6 us (84%)
  local copies, waits for them, and re-layouts  6.16 us (15%)
    pallas_call x1, Pallas kernels, per_device(): pl.pallas_call(functools.partial(kernel, n, m), out_shape=jax.ShapeDtypeS...  33.6 us
    unnamed x11, local copies, waits for them, and re-layouts  6.16 us

profile of v2, /device:TPU:1, one launch (start us, length us, event | category | flops | bytes accessed | tf_op | source)
XLA Modules:
  0.0 39.8 jit_solution(9311576999321545977)
XLA Ops:
  0.0 0.0 copy-start
  0.0 1.1 %copy-done = f32[1,1,512,384]{3,2,1,0:T(8,128)S(1)} copy-done((f32[1,1,512,384]{3,2,1,0:T(8,128)S(1)}, f32[1,1,512,384]{3,2,1,0:T(8,128)}, u32[]{:S(2)}) %copy-start) | copy-done | bytes 786456
  1.1 0.0 copy-start.1
  1.1 1.1 %copy-done.1 = f32[1,1,512,384]{3,2,1,0:T(8,128)S(1)} copy-done((f32[1,1,512,384]{3,2,1,0:T(8,128)S(1)}, f32[1,1,512,384]{3,2,1,0:T(8,128)}, u32[]{:S(2)}) %copy-start.1) | copy-done | bytes 786456
  2.3 0.0 copy-start.2
  2.3 1.1 %copy-done.2 = f32[1,1,384,384]{3,2,1,0:T(8,128)S(1)} copy-done((f32[1,1,384,384]{3,2,1,0:T(8,128)S(1)}, f32[1,1,384,384]{3,2,1,0:T(8,128)}, u32[]{:S(2)}) %copy-start.2) | copy-done | bytes 589848
  3.3 0.0 copy-start.3
  3.3 1.1 %copy-done.3 = f32[1,1,384,384]{3,2,1,0:T(8,128)S(1)} copy-done((f32[1,1,384,384]{3,2,1,0:T(8,128)S(1)}, f32[1,1,384,384]{3,2,1,0:T(8,128)}, u32[]{:S(2)}) %copy-start.3) | copy-done | bytes 589848
  4.4 0.0 copy-start.4
  4.4 0.9 %copy-done.4 = f32[1,48,384]{2,1,0:T(8,128)S(1)} copy-done((f32[1,48,384]{2,1,0:T(8,128)S(1)}, f32[1,48,384]{2,1,0:T(8,128)}, u32[]{:S(2)}) %copy-start.4) | copy-done | bytes 73752
  5.3 33.6 %shard_map.55 = f32[512,384]{1,0:T(8,128)S(1)} custom-call(f32[1,1,512,384]{3,2,1,0:T(8,128)S(1)} %copy-done, f32[1,1,512,384]{3,2,1,0:T(8,128)S(1)} %copy-done.1, f32[1,1,384,384]{3,2,1,0:T(8,128)S(1)} %copy-done.2, f32[1,1,384,384]{3,2,1,0:T(8,128)S(1)} %copy-done.3, f32[1,48,384]{2,1,0:T(8,128)S(1)} %copy-done.4), custom_call_target="tpu_custom_call" | custom-call | tf_op jit(solution)/shard_map/pallas_call | solution.py:187
  38.9 0.9 %copy.7 = f32[1,1,512,384]{3,2,1,0:T(8,128)} copy(f32[1,1,512,384]{3,2,1,0:T(8,128)S(1)} %bitcast.1) | data formatting | bytes 1572864
Async XLA Ops:
  0.0 1.1 %copy-start = (f32[1,1,512,384]{3,2,1,0:T(8,128)S(1)}, f32[1,1,512,384]{3,2,1,0:T(8,128)}, u32[]{:S(2)}) copy-start(f32[1,1,512,384]{3,2,1,0:T(8,128)} %b_hbm.1) | copy-start | bytes 2359300
  1.1 1.1 %copy-start.1 = (f32[1,1,512,384]{3,2,1,0:T(8,128)S(1)}, f32[1,1,512,384]{3,2,1,0:T(8,128)}, u32[]{:S(2)}) copy-start(f32[1,1,512,384]{3,2,1,0:T(8,128)} %q_hbm.1) | copy-start | bytes 2359300
  2.3 1.1 %copy-start.2 = (f32[1,1,384,384]{3,2,1,0:T(8,128)S(1)}, f32[1,1,384,384]{3,2,1,0:T(8,128)}, u32[]{:S(2)}) copy-start(f32[1,1,384,384]{3,2,1,0:T(8,128)} %r_hbm.1) | copy-start | bytes 1769476
  3.3 1.1 %copy-start.3 = (f32[1,1,384,384]{3,2,1,0:T(8,128)S(1)}, f32[1,1,384,384]{3,2,1,0:T(8,128)}, u32[]{:S(2)}) copy-start(f32[1,1,384,384]{3,2,1,0:T(8,128)} %m1_hbm.1) | copy-start | bytes 1769476
  4.4 0.9 %copy-start.4 = (f32[1,48,384]{2,1,0:T(8,128)S(1)}, f32[1,48,384]{2,1,0:T(8,128)}, u32[]{:S(2)}) copy-start(f32[1,48,384]{2,1,0:T(8,128)} %m2_hbm.1) | copy-start | bytes 221188

commit v3 on v2

--- a/solution.py
+++ b/solution.py
@@ -9,6 +9,7 @@
 
 MESH = pl.DeviceIdType.MESH
 TILE = 128
+VMEM_BYTES = 62 * 1024 * 1024
 f32 = jnp.float32
 bf16 = jnp.bfloat16
 
@@ -39,15 +40,21 @@
     b, q, r, m1, m2_parts, m2,
     bh, bl, bth, btl, qh, ql, rh, rl, m1h, m1l, m2h, m2l,
     wh, wl, ch, cl, dh, dl, th, tl, yh, yl,
-    packed, scatter, slab_sum, across, total,
-    load_sem, m2_send, m2_recv, rs_send, rs_recv, z_send, z_recv, ag_send, ag_recv,
+    packed, folded, grp_in, top_in, grp_sum, top_sum, total,
+    load_sem, own_send, own_recv, m2_send, m2_recv, pass_send, pass_recv, fold_send, fold_recv,
+    grp_send, grp_recv, top_send, top_recv, share_send, share_recv, last_send, last_recv,
 ):
     me = lax.axis_index("grp")
     my_top = lax.axis_index("top")
+    core = lax.rem(me, 2)
+    chip = me // 2
+    sibling = me + 1 - 2 * core
     width = m1.shape[0]
     blocks = width // TILE
     part = m2_parts.shape[1]
-    slab = slab_sum.shape[0]
+    half = packed.shape[0] // 2
+    grp_slab = grp_sum.shape[0]
+    top_slab = top_sum.shape[0]
 
     loads = [
         pltpu.make_async_copy(src, dst, load_sem.at[at])
@@ -64,36 +71,55 @@
     for load in loads:
         load.start()
 
+    def chip_peer(k):
+        return {"grp": 2 * lax.rem(chip + k, n // 2) + core}
+
+    def top_peer(k):
+        return {"top": lax.rem(my_top + k, m)}
+
+    other = {"grp": sibling}
     barrier = pltpu.get_barrier_semaphore()
-    for k in range(1, n):
-        pl.semaphore_signal(
-            barrier, inc=1, device_id={"grp": lax.rem(me + k, n)}, device_id_type=MESH
+    pl.semaphore_signal(barrier, inc=1, device_id=other, device_id_type=MESH)
+    for k in range(1, n // 2):
+        pl.semaphore_signal(barrier, inc=1, device_id=chip_peer(k), device_id_type=MESH)
+    for k in range(1, m):
+        pl.semaphore_signal(barrier, inc=1, device_id=top_peer(k), device_id_type=MESH)
+    pl.semaphore_wait(barrier, n // 2 + m - 1)
+
+    def remote(source, target, send, recv, peer):
+        return pltpu.make_async_remote_copy(
+            src_ref=source,
+            dst_ref=target,
+            send_sem=send,
+            recv_sem=recv,
+            device_id=peer,
+            device_id_type=MESH,
         )
-    for k in range(1, m):
-        pl.semaphore_signal(
-            barrier, inc=1, device_id={"top": lax.rem(my_top + k, m)}, device_id_type=MESH
-        )
-    pl.semaphore_wait(barrier, n + m - 2)
-
-    def spread(axis, at, size, source, target, send, recv):
-        copies = []
-        for k in range(1, size):
-            peer = lax.rem(at + k, size)
-            copy = pltpu.make_async_remote_copy(
-                src_ref=source(peer),
-                dst_ref=target(k),
-                send_sem=send.at[k - 1],
-                recv_sem=recv.at[k - 1],
-                device_id={axis: peer},
-                device_id_type=MESH,
-            )
+
+    def chips(source, target, send, recv):
+        return [
+            remote(source(lax.rem(chip + k, n // 2)), target(k), send.at[k - 1], recv.at[k - 1], chip_peer(k))
+            for k in range(1, n // 2)
+        ]
+
+    def tops(source, target, send, recv):
+        return [
+            remote(source(lax.rem(my_top + k, m)), target(k), send.at[k - 1], recv.at[k - 1], top_peer(k))
+            for k in range(1, m)
+        ]
+
+    def start(copies):
+        for copy in copies:
             copy.start()
-            copies.append(copy)
-        return copies
-
-    gather = spread(
-        "grp", me, n, lambda peer: m2_hbm.at[0], lambda k: m2_parts.at[me], m2_send, m2_recv
-    )
+
+    def finish(copies):
+        for copy in copies:
+            copy.wait_send()
+
+    gather = chips(lambda peer: m2_hbm.at[0], lambda k: m2_parts.at[me], m2_send, m2_recv)
+    start(gather)
+    own = remote(m2_hbm.at[0], m2_parts.at[me], own_send.at[0], own_recv.at[0], other)
+    own.start()
 
     loads[0].wait()
     split(b[...].T, bth, btl)
@@ -104,8 +130,20 @@
     split(m1[...], m1h, m1l)
     split(product((wh, wl), (m1h, m1l)), wh, wl)
 
+    passed = []
+    for k, copy in enumerate(gather):
+        copy.wait_recv()
+        came = 2 * lax.rem(chip + n // 2 - k - 1, n // 2) + core
+        passed.append(
+            remote(m2_parts.at[came], m2_parts.at[came], pass_send.at[k], pass_recv.at[k], other)
+        )
+        passed[-1].start()
+    loads[3].wait()
+    split(r[...], rh, rl)
+    split(b[...], bh, bl)
     loads[4].wait()
-    for copy in gather:
+    own.wait_recv()
+    for copy in passed:
         copy.wait_recv()
     for j in range(n):
         m2[j * part:(j + 1) * part, :] = m2_parts[j]
@@ -119,36 +157,102 @@
         for j in range(i + 1):
             packed[pl.ds((i * (i + 1) // 2 + j) * TILE, TILE), :] = row[:, j * TILE:(j + 1) * TILE]
 
-    def part_of(ref, at):
-        return ref.at[pl.ds(pl.multiple_of(at * slab, 8), slab), :]
-
-    reduce = spread(
-        "grp", me, n, lambda peer: part_of(packed, peer), lambda k: scatter.at[k - 1], rs_send, rs_recv
-    )
+    fold = remote(
+        packed.at[pl.ds(pl.multiple_of((1 - core) * half, 8), half), :],
+        folded,
+        fold_send.at[0],
+        fold_recv.at[0],
+        other,
+    )
+    fold.start()
+    mine = pl.ds(pl.multiple_of(core * half, 8), half)
+
+    def cut(ref, base, at, size):
+        return ref.at[pl.ds(pl.multiple_of(base + at * size, 8), size), :]
+
+    even_one = chips(
+        lambda peer: cut(packed, 0, peer, grp_slab), lambda k: grp_in.at[k - 1, pl.ds(0, grp_slab)], grp_send, grp_recv
+    )
+    even_two = tops(lambda peer: grp_sum, lambda k: top_in.at[k - 1, pl.ds(0, grp_slab)], top_send, top_recv)
+    even_three = chips(
+        lambda peer: cut(total, 0, chip, grp_slab), lambda k: cut(total, 0, chip, grp_slab), share_send, share_recv
+    )
+    odd_one = tops(
+        lambda peer: cut(packed, half, peer, top_slab), lambda k: top_in.at[k - 1, pl.ds(0, top_slab)], top_send, top_recv
+    )
+    odd_two = chips(lambda peer: top_sum, lambda k: grp_in.at[k - 1, pl.ds(0, top_slab)], grp_send, grp_recv)
+    odd_three = tops(
+        lambda peer: cut(total, half, my_top, top_slab), lambda k: cut(total, half, my_top, top_slab), share_send, share_recv
+    )
+
+    fold.wait()
+    packed[mine, :] += folded[...]
+
+    @pl.when(core == 0)
+    def _():
+        start(even_one)
+
+    @pl.when(core == 1)
+    def _():
+        start(odd_one)
+
     split(product((m1h, m1l), (m2h, m2l)), ch, cl)
-    value = packed[pl.ds(pl.multiple_of(me * slab, 8), slab), :]
-    for k, copy in enumerate(reduce):
-        copy.wait_recv()
-        value += scatter[k]
-    slab_sum[...] = value
-    over = spread(
-        "top", my_top, m, lambda peer: slab_sum, lambda k: across.at[k - 1], z_send, z_recv
-    )
+
+    @pl.when(core == 0)
+    def _():
+        value = packed[pl.ds(pl.multiple_of(chip * grp_slab, 8), grp_slab), :]
+        for k, copy in enumerate(even_one):
+            copy.wait_recv()
+            value += grp_in[k, :grp_slab]
+        grp_sum[...] = value
+        start(even_two)
+
+    @pl.when(core == 1)
+    def _():
+        value = packed[pl.ds(pl.multiple_of(half + my_top * top_slab, 8), top_slab), :]
+        for k, copy in enumerate(odd_one):
+            copy.wait_recv()
+            value += top_in[k, :top_slab]
+        top_sum[...] = value
+        start(odd_two)
+
     split(product((qh, ql), (ch, cl)), yh, yl)
-    for k, copy in enumerate(over):
-        copy.wait_recv()
-        value += across[k]
-    total[pl.ds(pl.multiple_of(me * slab, 8), slab), :] = value
-    share = spread(
-        "grp", me, n, lambda peer: part_of(total, me), lambda k: part_of(total, me), ag_send, ag_recv
-    )
-    loads[3].wait()
-    split(r[...], rh, rl)
+
+    @pl.when(core == 0)
+    def _():
+        value = grp_sum[...]
+        for k, copy in enumerate(even_two):
+            copy.wait_recv()
+            value += top_in[k, :grp_slab]
+        total[pl.ds(pl.multiple_of(chip * grp_slab, 8), grp_slab), :] = value
+        start(even_three)
+
+    @pl.when(core == 1)
+    def _():
+        value = top_sum[...]
+        for k, copy in enumerate(odd_two):
+            copy.wait_recv()
+            value += grp_in[k, :top_slab]
+        total[pl.ds(pl.multiple_of(half + my_top * top_slab, 8), top_slab), :] = value
+        start(odd_three)
+
     split(product((rh, rl), (ch, cl)), dh, dl)
-    split(b[...], bh, bl)
     o_ref[...] = product((bh, bl), (dh, dl), 1)
-    for copy in share:
-        copy.wait_recv()
+
+    last = remote(total.at[mine, :], total.at[mine, :], last_send.at[0], last_recv.at[0], other)
+
+    @pl.when(core == 0)
+    def _():
+        for copy in even_three:
+            copy.wait_recv()
+
+    @pl.when(core == 1)
+    def _():
+        for copy in odd_three:
+            copy.wait_recv()
+
+    last.start()
+    last.wait_recv()
 
     row_at = lax.broadcasted_iota(jnp.int32, (TILE, TILE), 0)
     column_at = lax.broadcasted_iota(jnp.int32, (TILE, TILE), 1)
@@ -165,9 +269,22 @@
     split(product((dh, dl), (th, tl)), wh, wl)
     o_ref[...] += product((yh, yl), (wh, wl), 1)
 
-    for copies in (gather, reduce, over, share):
-        for copy in copies:
-            copy.wait_send()
+    own.wait_send()
+    last.wait_send()
+    finish(gather)
+    finish(passed)
+
+    @pl.when(core == 0)
+    def _():
+        finish(even_one)
+        finish(even_two)
+        finish(even_three)
+
+    @pl.when(core == 1)
+    def _():
+        finish(odd_one)
+        finish(odd_two)
+        finish(odd_three)
 
 
 def per_device(n, m, basis_grad, leaf_q, leaf_rinv, merge_q1, merge_q2):
@@ -175,7 +292,10 @@
     part = merge_q2.shape[1]
     blocks = width // TILE
     length = blocks * (blocks + 1) // 2 * TILE
-    slab = length // n
+    half = length // 2
+    grp_slab = half // (n // 2)
+    top_slab = half // m
+    deep = max(grp_slab, top_slab)
     square, tall = (width, width), (rows, width)
 
     def pair(shape):
@@ -199,17 +319,23 @@
             *pair(tall), *pair((width, rows)), *pair(tall), *pair(square), *pair(square), *pair(square),
             *pair(square), *pair(square), *pair(square), *pair(square), *pair(tall),
             pltpu.VMEM((length, TILE), f32),
-            pltpu.VMEM((n - 1, slab, TILE), f32),
-            pltpu.VMEM((slab, TILE), f32),
-            pltpu.VMEM((m - 1, slab, TILE), f32),
+            pltpu.VMEM((half, TILE), f32),
+            pltpu.VMEM((n // 2 - 1, deep, TILE), f32),
+            pltpu.VMEM((m - 1, deep, TILE), f32),
+            pltpu.VMEM((grp_slab, TILE), f32),
+            pltpu.VMEM((top_slab, TILE), f32),
             pltpu.VMEM((length, TILE), f32),
             semaphores(5),
-            *[semaphores(n - 1)] * 4,
+            *[semaphores(1)] * 2,
+            *[semaphores(n // 2 - 1)] * 4,
+            *[semaphores(1)] * 2,
+            *[semaphores(n // 2 - 1)] * 2,
             *[semaphores(m - 1)] * 2,
-            *[semaphores(n - 1)] * 2,
+            *[semaphores(max(n // 2, m) - 1)] * 2,
+            *[semaphores(1)] * 2,
         ],
         compiler_params=pltpu.CompilerParams(
-            collective_id=0, has_side_effects=True, vmem_limit_bytes=48 * 1024 * 1024
+            collective_id=0, has_side_effects=True, vmem_limit_bytes=VMEM_BYTES
         ),
     )(basis_grad, leaf_q, leaf_rinv, merge_q1, merge_q2)
     return result[None, None]

time: 40.2 us -> 31.4 us (0.78)
  Pallas kernels: 33.6 us -> 29.2 us
  local copies, waits for them, and re-layouts: 6.16 us -> 2.06 us
    pallas_call x1, Pallas kernels: 33.6 us -> 29.2 us  [per_device(): pl.pallas_call(functools.partial(kernel, n, m), out_shape=jax.ShapeDtypeS...]
    unnamed x11 -> x1, local copies, waits for them, and re-layouts: 6.16 us -> 2.06 us
where the time goes in v3:
time: 31.4 us; the launch traced here: 31.3 us
  Pallas kernels  29.2 us (93%)
  local copies, waits for them, and re-layouts  2.06 us (7%)
    pallas_call x1, Pallas kernels, per_device(): pl.pallas_call(functools.partial(kernel, n, m), out_shape=jax.ShapeDtypeS...  29.2 us
    unnamed x1, local copies, waits for them, and re-layouts  2.06 us

profile of v3, /device:TPU:1, one launch (start us, length us, event | category | flops | bytes accessed | tf_op | source)
XLA Modules:
  0.0 31.3 jit_solution(5648832771941374942)
XLA Ops:
  0.0 29.2 %shard_map.55 = f32[512,384]{1,0:T(8,128)} custom-call(f32[1,1,512,384]{3,2,1,0:T(8,128)} %b_hbm.1, f32[1,1,512,384]{3,2,1,0:T(8,128)} %q_hbm.1, f32[1,1,384,384]{3,2,1,0:T(8,128)} %r_hbm.1, f32[1,1,384,384]{3,2,1,0:T(8,128)} %m1_hbm.1, f32[1,48,384]{2,1,0:T(8,128)} %m2_hbm.1), custom_call_target="tpu_custom_call" | custom-call | tf_op jit(solution)/shard_map/pallas_call | solution.py:307
  29.2 2.1 %copy.7 = f32[1,1,512,384]{3,2,1,0:T(8,128)} copy(f32[1,1,512,384]{3,2,1,0:T(8,128)} %bitcast.1) | data formatting | bytes 1572864

commit v4 on v3

--- a/solution.py
+++ b/solution.py
@@ -9,7 +9,7 @@
 
 MESH = pl.DeviceIdType.MESH
 TILE = 128
-VMEM_BYTES = 62 * 1024 * 1024
+VMEM_BYTES = 48 * 1024 * 1024
 f32 = jnp.float32
 bf16 = jnp.bfloat16
 
@@ -40,7 +40,7 @@
     b, q, r, m1, m2_parts, m2,
     bh, bl, bth, btl, qh, ql, rh, rl, m1h, m1l, m2h, m2l,
     wh, wl, ch, cl, dh, dl, th, tl, yh, yl,
-    packed, folded, grp_in, top_in, grp_sum, top_sum, total,
+    packed, mixed, folded, grp_in, top_in, grp_sum, top_sum, total,
     load_sem, own_send, own_recv, m2_send, m2_recv, pass_send, pass_recv, fold_send, fold_recv,
     grp_send, grp_recv, top_send, top_recv, share_send, share_recv, last_send, last_recv,
 ):
@@ -128,7 +128,19 @@
     split(product((bth, btl), (qh, ql)), wh, wl)
     loads[2].wait()
     split(m1[...], m1h, m1l)
-    split(product((wh, wl), (m1h, m1l)), wh, wl)
+    mixed[...] = product((wh, wl), (m1h, m1l))
+    cells = [(i, j) for i in range(blocks) for j in range(i + 1)]
+    sides = cells[:len(cells) // 2], cells[len(cells) // 2:]
+    spans = [pl.ds(side[0][0] * TILE, (side[-1][0] - side[0][0] + 1) * TILE) for side in sides]
+    folds = [
+        remote(mixed.at[span], folded.at[span], fold_send.at[0], fold_recv.at[0], other)
+        for span in reversed(spans)
+    ]
+    for at in range(2):
+        @pl.when(core == at)
+        def _():
+            folds[at].start()
+
 
     passed = []
     for k, copy in enumerate(gather):
@@ -148,24 +160,23 @@
     for j in range(n):
         m2[j * part:(j + 1) * part, :] = m2_parts[j]
     split(m2[...], m2h, m2l)
-    for i in range(blocks):
-        rows = pl.ds(i * TILE, TILE)
-        columns = pl.ds(0, (i + 1) * TILE)
-        row = product(
-            (wh.at[rows, :], wl.at[rows, :]), (m2h.at[:, columns], m2l.at[:, columns])
-        )
-        for j in range(i + 1):
-            packed[pl.ds((i * (i + 1) // 2 + j) * TILE, TILE), :] = row[:, j * TILE:(j + 1) * TILE]
-
-    fold = remote(
-        packed.at[pl.ds(pl.multiple_of((1 - core) * half, 8), half), :],
-        folded,
-        fold_send.at[0],
-        fold_recv.at[0],
-        other,
-    )
-    fold.start()
-    mine = pl.ds(pl.multiple_of(core * half, 8), half)
+    for at in range(2):
+        @pl.when(core == at)
+        def _():
+            folds[at].wait_send()
+            folds[1 - at].wait_recv()
+            split(mixed[spans[at]] + folded[spans[at]], wh.at[spans[at]], wl.at[spans[at]])
+            for i in sorted({cell[0] for cell in sides[at]}):
+                line = [cell[1] for cell in sides[at] if cell[0] == i]
+                rows = pl.ds(i * TILE, TILE)
+                columns = pl.ds(line[0] * TILE, len(line) * TILE)
+                row = product(
+                    (wh.at[rows, :], wl.at[rows, :]), (m2h.at[:, columns], m2l.at[:, columns])
+                )
+                for j in line:
+                    packed[pl.ds(cells.index((i, j)) * TILE, TILE), :] = row[
+                        :, (j - line[0]) * TILE:(j - line[0] + 1) * TILE
+                    ]
 
     def cut(ref, base, at, size):
         return ref.at[pl.ds(pl.multiple_of(base + at * size, 8), size), :]
@@ -185,8 +196,22 @@
         lambda peer: cut(total, half, my_top, top_slab), lambda k: cut(total, half, my_top, top_slab), share_send, share_recv
     )
 
-    fold.wait()
-    packed[mine, :] += folded[...]
+    even_last = [
+        remote(
+            cut(total, 0, lax.rem(chip + n // 2 - k, n // 2), grp_slab),
+            cut(total, 0, lax.rem(chip + n // 2 - k, n // 2), grp_slab),
+            last_send.at[k], last_recv.at[k], other,
+        )
+        for k in range(n // 2)
+    ]
+    odd_last = [
+        remote(
+            cut(total, half, lax.rem(my_top + m - k, m), top_slab),
+            cut(total, half, lax.rem(my_top + m - k, m), top_slab),
+            last_send.at[k], last_recv.at[k], other,
+        )
+        for k in range(m)
+    ]
 
     @pl.when(core == 0)
     def _():
@@ -226,6 +251,7 @@
             value += top_in[k, :grp_slab]
         total[pl.ds(pl.multiple_of(chip * grp_slab, 8), grp_slab), :] = value
         start(even_three)
+        even_last[0].start()
 
     @pl.when(core == 1)
     def _():
@@ -235,24 +261,26 @@
             value += grp_in[k, :top_slab]
         total[pl.ds(pl.multiple_of(half + my_top * top_slab, 8), top_slab), :] = value
         start(odd_three)
+        odd_last[0].start()
 
     split(product((rh, rl), (ch, cl)), dh, dl)
     o_ref[...] = product((bh, bl), (dh, dl), 1)
 
-    last = remote(total.at[mine, :], total.at[mine, :], last_send.at[0], last_recv.at[0], other)
-
-    @pl.when(core == 0)
-    def _():
-        for copy in even_three:
-            copy.wait_recv()
-
-    @pl.when(core == 1)
-    def _():
-        for copy in odd_three:
-            copy.wait_recv()
-
-    last.start()
-    last.wait_recv()
+    @pl.when(core == 0)
+    def _():
+        for k, copy in enumerate(even_three):
+            copy.wait_recv()
+            even_last[k + 1].start()
+        for copy in odd_last:
+            copy.wait_recv()
+
+    @pl.when(core == 1)
+    def _():
+        for k, copy in enumerate(odd_three):
+            copy.wait_recv()
+            odd_last[k + 1].start()
+        for copy in even_last:
+            copy.wait_recv()
 
     row_at = lax.broadcasted_iota(jnp.int32, (TILE, TILE), 0)
     column_at = lax.broadcasted_iota(jnp.int32, (TILE, TILE), 1)
@@ -270,7 +298,6 @@
     o_ref[...] += product((yh, yl), (wh, wl), 1)
 
     own.wait_send()
-    last.wait_send()
     finish(gather)
     finish(passed)
 
@@ -279,12 +306,14 @@
         finish(even_one)
         finish(even_two)
         finish(even_three)
+        finish(even_last)
 
     @pl.when(core == 1)
     def _():
         finish(odd_one)
         finish(odd_two)
         finish(odd_three)
+        finish(odd_last)
 
 
 def per_device(n, m, basis_grad, leaf_q, leaf_rinv, merge_q1, merge_q2):
@@ -304,6 +333,10 @@
     def semaphores(count):
         return pltpu.SemaphoreType.DMA((max(count, 1),))
 
+    basis_grad, leaf_q, leaf_rinv, merge_q1, merge_q2 = (
+        pltpu.with_memory_space_constraint(value, pltpu.HBM)
+        for value in (basis_grad, leaf_q, leaf_rinv, merge_q1, merge_q2)
+    )
     result = pl.pallas_call(
         functools.partial(kernel, n, m),
         out_shape=jax.ShapeDtypeStruct(tall, f32),
@@ -319,7 +352,8 @@
             *pair(tall), *pair((width, rows)), *pair(tall), *pair(square), *pair(square), *pair(square),
             *pair(square), *pair(square), *pair(square), *pair(square), *pair(tall),
             pltpu.VMEM((length, TILE), f32),
-            pltpu.VMEM((half, TILE), f32),
+            pltpu.VMEM(square, f32),
+            pltpu.VMEM(square, f32),
             pltpu.VMEM((n // 2 - 1, deep, TILE), f32),
             pltpu.VMEM((m - 1, deep, TILE), f32),
             pltpu.VMEM((grp_slab, TILE), f32),
@@ -332,7 +366,7 @@
             *[semaphores(n // 2 - 1)] * 2,
             *[semaphores(m - 1)] * 2,
             *[semaphores(max(n // 2, m) - 1)] * 2,
-            *[semaphores(1)] * 2,
+            *[semaphores(max(n // 2, m))] * 2,
         ],
         compiler_params=pltpu.CompilerParams(
             collective_id=0, has_side_effects=True, vmem_limit_bytes=VMEM_BYTES

time: 31.4 us -> 27.3 us (0.87)
  Pallas kernels: 29.2 us -> 26.3 us
  local copies, waits for them, and re-layouts: 2.06 us -> 0.88 us
    pallas_call x1, Pallas kernels: 29.2 us -> 26.3 us  [per_device(): pl.pallas_call(functools.partial(kernel, n, m), out_shape=jax.ShapeDtypeS...]
    unnamed x1, local copies, waits for them, and re-layouts: 2.06 us -> 0.88 us
where the time goes in v4:
time: 27.3 us; the launch traced here: 27.2 us
  Pallas kernels  26.3 us (96%)
  local copies, waits for them, and re-layouts  0.88 us (3%)
    pallas_call x1, Pallas kernels, per_device(): pl.pallas_call(functools.partial(kernel, n, m), out_shape=jax.ShapeDtypeS...  26.3 us
    unnamed x1, local copies, waits for them, and re-layouts  0.88 us

profile of v4, /device:TPU:1, one launch (start us, length us, event | category | flops | bytes accessed | tf_op | source)
XLA Modules:
  0.0 27.2 jit_solution(7047959362330629707)
XLA Ops:
  0.0 26.3 %shard_map.55 = f32[512,384]{1,0:T(8,128)S(1)} custom-call(f32[1,1,512,384]{3,2,1,0:T(8,128)} %b_hbm.1, f32[1,1,512,384]{3,2,1,0:T(8,128)} %q_hbm.1, f32[1,1,384,384]{3,2,1,0:T(8,128)} %r_hbm.1, f32[1,1,384,384]{3,2,1,0:T(8,128)} %m1_hbm.1, f32[1,48,384]{2,1,0:T(8,128)} %m2_hbm.1), custom_call_target="tpu_custom_call" | custom-call | tf_op jit(solution)/shard_map/pallas_call | solution.py:340
  26.3 0.9 %copy.7 = f32[1,1,512,384]{3,2,1,0:T(8,128)} copy(f32[1,1,512,384]{3,2,1,0:T(8,128)S(1)} %bitcast.1) | data formatting | bytes 1572864

commit v5 on v4

--- a/solution.py
+++ b/solution.py
@@ -29,9 +29,10 @@
 def product(former, latter, latter_dim=0):
     former_high, former_low = former
     latter_high, latter_low = latter
-    total = dot(former_high[...], latter_low[...], latter_dim)
-    total += dot(former_low[...], latter_high[...], latter_dim)
-    return total + dot(former_high[...], latter_high[...], latter_dim)
+    high, other = former_high[...], latter_high[...]
+    left = jnp.concatenate([high, former_low[...], high], axis=1)
+    right = jnp.concatenate([latter_low[...], other, other], axis=latter_dim)
+    return dot(left, right, latter_dim)
 
 
 def kernel(
@@ -266,27 +267,12 @@
     split(product((rh, rl), (ch, cl)), dh, dl)
     o_ref[...] = product((bh, bl), (dh, dl), 1)
 
-    @pl.when(core == 0)
-    def _():
-        for k, copy in enumerate(even_three):
-            copy.wait_recv()
-            even_last[k + 1].start()
-        for copy in odd_last:
-            copy.wait_recv()
-
-    @pl.when(core == 1)
-    def _():
-        for k, copy in enumerate(odd_three):
-            copy.wait_recv()
-            odd_last[k + 1].start()
-        for copy in even_last:
-            copy.wait_recv()
-
     row_at = lax.broadcasted_iota(jnp.int32, (TILE, TILE), 0)
     column_at = lax.broadcasted_iota(jnp.int32, (TILE, TILE), 1)
-    for i in range(blocks):
-        for j in range(i + 1):
-            block = -total[pl.ds((i * (i + 1) // 2 + j) * TILE, TILE), :]
+
+    def assemble(side):
+        for i, j in side:
+            block = -total[pl.ds(cells.index((i, j)) * TILE, TILE), :]
             if i == j:
                 block = jnp.where(row_at >= column_at, block, block.T)
             here = (pl.ds(i * TILE, TILE), pl.ds(j * TILE, TILE))
@@ -294,6 +280,27 @@
             if i != j:
                 there = (pl.ds(j * TILE, TILE), pl.ds(i * TILE, TILE))
                 split(block.T, th.at[there], tl.at[there])
+
+    @pl.when(core == 0)
+    def _():
+        for k, copy in enumerate(even_three):
+            copy.wait_recv()
+            even_last[k + 1].start()
+        assemble(sides[0])
+        for copy in odd_last:
+            copy.wait_recv()
+        assemble(sides[1])
+
+    @pl.when(core == 1)
+    def _():
+        for k, copy in enumerate(odd_three):
+            copy.wait_recv()
+            odd_last[k + 1].start()
+        assemble(sides[1])
+        for copy in even_last:
+            copy.wait_recv()
+        assemble(sides[0])
+
     split(product((dh, dl), (th, tl)), wh, wl)
     o_ref[...] += product((yh, yl), (wh, wl), 1)
 

time: 27.3 us -> 27 us (0.989)
  Pallas kernels: 26.3 us -> 26 us
    pallas_call x1, Pallas kernels: 26.3 us -> 26 us  [per_device(): pl.pallas_call(functools.partial(kernel, n, m), out_shape=jax.ShapeDtypeS...]
where the time goes in v5:
time: 27 us; the launch traced here: 26.9 us
  Pallas kernels  26 us (96%)
  local copies, waits for them, and re-layouts  0.88 us (3%)
    pallas_call x1, Pallas kernels, per_device(): pl.pallas_call(functools.partial(kernel, n, m), out_shape=jax.ShapeDtypeS...  26 us
    unnamed x1, local copies, waits for them, and re-layouts  0.88 us

profile of v5, /device:TPU:1, one launch (start us, length us, event | category | flops | bytes accessed | tf_op | source)
XLA Modules:
  0.0 26.9 jit_solution(12623376399560706468)
XLA Ops:
  0.0 26.0 %shard_map.55 = f32[512,384]{1,0:T(8,128)S(1)} custom-call(f32[1,1,512,384]{3,2,1,0:T(8,128)} %b_hbm.1, f32[1,1,512,384]{3,2,1,0:T(8,128)} %q_hbm.1, f32[1,1,384,384]{3,2,1,0:T(8,128)} %r_hbm.1, f32[1,1,384,384]{3,2,1,0:T(8,128)} %m1_hbm.1, f32[1,48,384]{2,1,0:T(8,128)} %m2_hbm.1), custom_call_target="tpu_custom_call" | custom-call | tf_op jit(solution)/shard_map/pallas_call | solution.py:347
  26.0 0.9 %copy.7 = f32[1,1,512,384]{3,2,1,0:T(8,128)} copy(f32[1,1,512,384]{3,2,1,0:T(8,128)S(1)} %bitcast.1) | data formatting | bytes 1572864
